TPU v7x, 32 devices: a whole 2x2x4 slice. The times are simulated.
32 devices in a mesh: seq: 4 (over y, core), user: 8 (over z, x).
Axes of the slice: x: 2, y: 2, z: 4, core: 2. Of those that a mesh axis runs over, the one named last changes fastest.
Arguments:
- history: bfloat16 [8, 2048, 256], P('user', 'seq'), may hold values from -6 to 6
- cotangent: bfloat16 [8, 2048, 256], P('user', 'seq'), may hold values from -6 to 6
- weights: bfloat16 [4, 3, 256, 256], replicated, may hold values from -0.21875 to 0.21875
- ln_gain: float32 [4, 256], replicated, may hold values from 0.1 to 1.9
- conv_bias: float32 [4, 256], replicated, may hold values from -3 to 3
- pooled_grad: bfloat16 [8, 64, 128], P('user', 'seq'), may hold values from -6 to 6
- table_owner: int32 [64], P('seq'), may hold values from 0 to 7, as said below
- row_ids: int32 [8, 64], P('user', 'seq'), may hold values from 0 to 999999
Outputs:
- d_history: bfloat16 [8, 2048, 256], P('user', 'seq')
- grad_weights: float32 [4, 3, 256, 256], replicated
- grad_gain: float32 [4, 256], replicated
- grad_bias: float32 [4, 256], replicated
- table_grad: float32 [64, 8, 128], P(('seq', 'user'))
Inputs may be any that keep to these rules, and one draw needn't show every extreme that they name: `table_owner`: within each block of 16 consecutive tables, every user index owns exactly 2 tables.
All inputs are finite; a program needn't handle non-finite values.
Results may differ from a plain program's by a relative error of at most 0.0095.
Values may be sent and summed in bfloat16 or wider, within the bound.
A program may use at most 64 MiB of HBM per device.

v0:
```python
import math

import jax
import jax.numpy as jnp
from jax import lax
from jax.sharding import PartitionSpec as P

TAPS = 3
LAYERS = 4


epsilon = 1e-05


def passed_along(block, axis, distance):
    devices = range(lax.axis_size(axis))
    route = [(i - distance, i) for i in devices if i - distance in devices]
    return lax.ppermute(block, axis, route)


def gelu_tanh(values):
    return jax.nn.gelu(values, approximate=True)


def gelu_slope(values, upstream):
    return jax.vjp(gelu_tanh, values)[1](upstream)[0]


def normalize(resid_field):
    center = resid_field - jnp.mean(resid_field, -1, keepdims=True)
    inverse = lax.rsqrt(jnp.mean(center * center, -1, keepdims=True) + epsilon)
    return (center * inverse, inverse)


def dilated(padded, kernel, shift_bias, dilation):
    user_count, total_len, channels = padded.shape
    out_len = total_len - (TAPS - 1) * dilation
    result = jnp.zeros((user_count * out_len, kernel.shape[2]), jnp.float32) + shift_bias
    for tap_index in range(TAPS):
        offset = (TAPS - 1 - tap_index) * dilation
        window = padded[:, offset : offset + out_len].reshape(user_count * out_len, channels)
        result = result + jnp.dot(window, kernel[tap_index], preferred_element_type=jnp.float32)
    return result.reshape(user_count, out_len, kernel.shape[2])


def coalesce(pieces):
    got_rows, got_ids = pieces
    per_owner = got_rows.shape[2]
    flat_rows = got_rows.reshape(got_rows.shape[0], per_owner, got_rows.shape[3])
    key_grid = got_ids.reshape(got_ids.shape[0], per_owner).T
    matches = (key_grid[:, :, None] == key_grid[:, None, :]).astype(jnp.bfloat16)
    return jnp.einsum("tuv,vte->tue", matches, flat_rows, preferred_element_type=jnp.float32)


def body(history, cotangent, weights, ln_gain, conv_bias, pooled_grad, table_owner, row_ids):
    user_count, length, channels = history.shape
    row_count = user_count * length
    stored = []
    resid_field = history.astype(jnp.float32)
    for layer_num in range(LAYERS):
        dilation = 2**layer_num
        lookback = (TAPS - 1) * dilation
        normed, inverse = normalize(resid_field)
        hidden = gelu_tanh(normed * ln_gain[layer_num]).astype(jnp.bfloat16)
        border = passed_along(hidden[:, length - lookback :], "seq", 1)
        padded = jnp.concatenate([border, hidden], 1)
        stored.append((resid_field, padded))
        resid_field = resid_field + dilated(
            padded, weights[layer_num], conv_bias[layer_num], dilation
        )
    grad_flow = cotangent.astype(jnp.float32)
    weight_terms = [None] * LAYERS
    gain_terms = [None] * LAYERS
    bias_terms = [None] * LAYERS
    for layer_num in reversed(range(LAYERS)):
        dilation = 2**layer_num
        lookback = (TAPS - 1) * dilation
        field_in, padded = stored[layer_num]
        flow_half = grad_flow.astype(jnp.bfloat16)
        flow_flat = flow_half.reshape(row_count, channels)
        bias_terms[layer_num] = jnp.sum(grad_flow, (0, 1))
        tap_terms = []
        for tap_index in range(TAPS):
            offset = lookback - tap_index * dilation
            window = padded[:, offset : offset + length].reshape(row_count, channels)
            tap_terms.append(
                lax.dot_general(
                    window, flow_flat, (((0,), (0,)), ((), ())), preferred_element_type=jnp.float32
                )
            )
        weight_terms[layer_num] = jnp.stack(tap_terms)
        future = passed_along(flow_half[:, :lookback], "seq", -1)
        extended = jnp.concatenate([flow_half, future], 1)
        backward = jnp.zeros((row_count, channels), jnp.float32)
        for tap_index in range(TAPS):
            offset = tap_index * dilation
            window = extended[:, offset : offset + length].reshape(row_count, channels)
            backward = backward + lax.dot_general(
                window,
                weights[layer_num, tap_index],
                (((1,), (1,)), ((), ())),
                preferred_element_type=jnp.float32,
            )
        normed, inverse = normalize(field_in)
        slopes = gelu_slope(
            normed * ln_gain[layer_num], backward.reshape(user_count, length, channels)
        )
        gain_terms[layer_num] = jnp.sum(slopes * normed, (0, 1))
        scaled = slopes * ln_gain[layer_num]
        grad_flow = grad_flow + inverse * (
            scaled
            - jnp.mean(scaled, -1, keepdims=True)
            - normed * jnp.mean(scaled * normed, -1, keepdims=True)
        )
    weight_local = jnp.stack(weight_terms)
    gain_local = jnp.stack(gain_terms)
    bias_local = jnp.stack(bias_terms)
    weight_total, gain_total, bias_total = lax.psum(
        (weight_local, gain_local, bias_local), ("seq", "user")
    )
    factor = 1.0 / math.sqrt(user_count * lax.axis_size("user") * length * lax.axis_size("seq"))
    listing = jnp.argsort(table_owner, stable=True)
    per_owner = listing.shape[0] // lax.axis_size("user")
    send_rows = jnp.take(pooled_grad, listing, axis=1).reshape(
        user_count, lax.axis_size("user"), per_owner, pooled_grad.shape[2]
    )
    send_ids = jnp.take(row_ids, listing, axis=1).reshape(
        user_count, lax.axis_size("user"), per_owner
    )
    table_grad = coalesce(
        (
            lax.all_to_all(send_rows, "user", split_axis=1, concat_axis=0, tiled=True),
            lax.all_to_all(send_ids, "user", split_axis=1, concat_axis=0, tiled=True),
        )
    )
    return (
        grad_flow.astype(jnp.bfloat16),
        weight_total * factor,
        gain_total * factor,
        bias_total * factor,
        table_grad,
    )


def solution(mesh):
    in_specs = (
        P("user", "seq", None),
        P("user", "seq", None),
        P(),
        P(),
        P(),
        P("user", "seq", None),
        P("seq"),
        P("user", "seq"),
    )
    out_specs = (P("user", "seq", None), P(), P(), P(), P(("seq", "user"), None, None))
    return jax.shard_map(body, mesh=mesh, in_specs=in_specs, out_specs=out_specs, check_vma=False)
```

profile of v0, /device:TPU:0, one launch (start us, length us, event | category | flops | bytes accessed | tf_op | source)
XLA Modules:
  0.0 236.2 jit_solution(5344520800691517173)
XLA Ops:
  7.2 0.8 fusion.190
  8.0 1.1 convert_reduce_fusion
  9.2 1.2 fusion.30
  10.3 1.3 fusion.21
  11.6 2.4 %collective-permute-start = (bf16[1,2,256]{2,1,0:T(2,128)(2,1)S(1)}, bf16[1,2,256]{2,1,0:T(2,128)(2,1)S(1)}, u32[]{:S(2)}, u32[]{:S(2)}) collective-permute-start(bf16[1,2,256]{2,1,0:T(2,128)(2,1)S(1)} %slice.220), channel_id=1, source_target_pairs={{0,8},{8,16},{16,24},{1,9},{9,17},{17,25},{2,10},{10,18},{18,26},{... | collective-permute-start | bytes 3080 | tf_op jit(solution)/shard_map/ppermute | solution.py:18
  14.0 0.7 slice.198
  14.7 1.3 collective-permute-start.3
  16.0 1.9 sort.17
  17.9 1.3 gather_fusion
  19.3 0.7 reshape.430
  19.9 6.6 %all-to-all-start = ((s32[1,8,2]{2,0,1:T(1,128)}), s32[1,8,2]{2,0,1:T(1,128)S(1)}, u32[]{:S(2)}, u32[]{:S(2)}) async-start(s32[1,8,2]{2,0,1:T(1,128)} %bitcast.75), calls=%async_computation | async-start | bytes 8192 | tf_op jit(solution)/shard_map/all_to_all | solution.py:133
  26.6 1.2 fusion.104
  27.8 1.2 convolution_add_fusion.16
  29.6 0.7 fusion.162
  30.3 0.7 constant_dynamic-update-slice_fusion.1
  31.0 2.0 all-to-all-done
  33.0 4.0 %all-to-all-start.1 = ((bf16[1,8,2,128]{3,2,0,1:T(2,128)(2,1)}), bf16[1,8,2,128]{3,2,0,1:T(2,128)(2,1)S(1)}, u32[]{:S(2)}, u32[]{:S(2)}) async-start(bf16[1,8,2,128]{3,2,0,1:T(2,128)(2,1)} %fusion.162), calls=%async_computation.1 | async-start | bytes 8192 | tf_op jit(solution)/shard_map/all_to_all | solution.py:132
  37.2 1.1 convolution_add_fusion.15
  38.3 1.3 fusion.192
  40.1 3.5 %collective-permute-start.1 = (bf16[1,4,256]{2,1,0:T(4,128)(2,1)S(1)}, bf16[1,4,256]{2,1,0:T(4,128)(2,1)S(1)}, u32[]{:S(2)}, u32[]{:S(2)}) collective-permute-start(bf16[1,4,256]{2,1,0:T(4,128)(2,1)S(1)} %slice.223), channel_id=1, source_target_pairs={{0,8},{8,16},{16,24},{1,9},{9,17},{17,25},{2,10},{10,18},{18,26},{... | collective-permute-start | bytes 6152 | tf_op jit(solution)/shard_map/ppermute | solution.py:18
  43.7 1.1 convolution_add_fusion.13
  44.8 1.1 convolution_add_fusion.12
  46.0 1.3 fusion.193
  47.8 4.5 %collective-permute-start.2 = (bf16[1,8,256]{2,1,0:T(8,128)(2,1)S(1)}, bf16[1,8,256]{2,1,0:T(8,128)(2,1)S(1)}, u32[]{:S(2)}, u32[]{:S(2)}) collective-permute-start(bf16[1,8,256]{2,1,0:T(8,128)(2,1)S(1)} %slice.226), channel_id=1, source_target_pairs={{0,8},{8,16},{16,24},{1,9},{9,17},{17,25},{2,10},{10,18},{18,26},{... | collective-permute-start | bytes 12296 | tf_op jit(solution)/shard_map/ppermute | solution.py:18
  52.3 1.1 convolution_add_fusion.10
  53.4 1.1 convolution_add_fusion.9
  54.6 1.2 fusion.194
  56.1 0.8 fusion.160
  56.9 0.6 constant_dynamic-update-slice_fusion
  57.5 1.2 convolution_add_fusion.7
  58.8 1.8 multiply_reduce_fusion
  61.0 0.9 copy-done.3
  62.8 1.3 collective-permute-start.4
  64.1 4.3 %collective-permute-start.7 = (bf16[1,16,256]{2,1,0:T(8,128)(2,1)S(1)}, bf16[1,16,256]{2,1,0:T(8,128)(2,1)S(1)}, u32[]{:S(2)}, u32[]{:S(2)}) collective-permute-start(bf16[1,16,256]{2,1,0:T(8,128)(2,1)S(1)} %slice.240), channel_id=1, source_target_pairs={{0,8},{8,16},{16,24},{1,9},{9,17},{17,25},{2,10},{10,18},{18,26},{... | collective-permute-start | bytes 24584 | tf_op jit(solution)/shard_map/ppermute | solution.py:18
  69.3 0.8 multiply_reduce_fusion.1
  71.1 1.3 collective-permute-start.5
  73.0 2.5 %collective-permute-done.5 = bf16[1,4,256]{2,1,0:T(4,128)(2,1)S(1)} collective-permute-done((bf16[1,4,256]{2,1,0:T(4,128)(2,1)S(1)}, bf16[1,4,256]{2,1,0:T(4,128)(2,1)S(1)}, u32[]{:S(2)}, u32[]{:S(2)}) %collective-permute-start.5) | collective-permute-done | bytes 2080 | tf_op jit(solution)/shard_map/ppermute | solution.py:18
  75.7 0.8 multiply_reduce_fusion.2
  77.5 1.5 collective-permute-start.6
  80.2 2.1 pad_maximum_fusion
  82.4 1.2 convolution_add_fusion.1
  83.6 1.7 fusion.29
  85.3 44.3 %all-reduce = (f32[4,256]{1,0:T(4,128)S(1)}, f32[4,256]{1,0:T(4,128)S(1)}) all-reduce(f32[4,256]{1,0:T(4,128)S(1)} %pad_maximum_fusion.8, f32[4,256]{1,0:T(4,128)S(1)} %pad_maximum_fusion.9), channel_id=1, replica_groups=mesh['seq'=4,'user'=8] {'seq','user'}, use_global_device_ids=true, to_apply=%region_21.0 | all-reduce | flops 2048 | bytes 16384 | tf_op jit(solution)/shard_map/psum | solution.py:118
  129.6 0.6 broadcast_multiply_fusion.2
  130.2 0.6 broadcast_multiply_fusion.1
  130.8 1.0 fusion.28
  131.8 93.8 %all-reduce.3.cloned.1.call-done = f32[4,3,256,256]{3,2,1,0:T(8,128)} async-done(((f32[4,3,256,256]{3,2,1,0:T(8,128)}), f32[4,3,256,256]{3,2,1,0:T(8,128)}) %all-reduce.3.cloned.1.call-update) | async-done | bytes 3145744 | tf_op jit(solution)/shard_map/psum | solution.py:118
  225.6 3.8 %broadcast_multiply_fusion = f32[4,3,256,256]{3,2,1,0:T(8,128)} fusion(f32[4,3,256,256]{3,2,1,0:T(8,128)} %all-reduce.3.cloned.1.call-done), kind=kLoop, calls=%fused_computation.3 | loop fusion | flops 786432 | bytes 6291456 | tf_op jit(solution)/shard_map/mul | solution.py:138
  (83 shorter events, 8.4 us)
Async XLA Ops:
  7.2 21.8 %copy-start = (bf16[1,16,128]{2,1,0:T(8,128)(2,1)S(1)}, bf16[1,16,128]{2,1,0:T(8,128)(2,1)}, u32[]{:S(2)}) copy-start(bf16[1,16,128]{2,1,0:T(8,128)(2,1)} %param.13) | copy-start | bytes 12292
  7.2 19.4 %copy-start.2 = (bf16[1,512,256]{2,1,0:T(8,128)(2,1)S(1)}, bf16[1,512,256]{2,1,0:T(8,128)(2,1)}, u32[]{:S(2)}) copy-start(bf16[1,512,256]{2,1,0:T(8,128)(2,1)} %param.9) | copy-start | bytes 786436
  7.2 19.4 %copy-start.4 = (f32[4,256]{1,0:T(4,128)S(1)}, f32[4,256]{1,0:T(4,128)}, u32[]{:S(2)}) copy-start(f32[4,256]{1,0:T(4,128)} %param.12) | copy-start | bytes 12292
  11.6 25.5 %collective-permute-start = (bf16[1,2,256]{2,1,0:T(2,128)(2,1)S(1)}, bf16[1,2,256]{2,1,0:T(2,128)(2,1)S(1)}, u32[]{:S(2)}, u32[]{:S(2)}) collective-permute-start(bf16[1,2,256]{2,1,0:T(2,128)(2,1)S(1)} %slice.220), channel_id=1, source_target_pairs={{0,8},{8,16},{16,24},{1,9},{9,17},{17,25},{2,10},{10,18},{18,26},{... | collective-permute-start | bytes 3080 | tf_op jit(solution)/shard_map/ppermute | solution.py:18
  14.7 42.2 %collective-permute-start.3 = (bf16[1,16,256]{2,1,0:T(8,128)(2,1)S(1)}, bf16[1,16,256]{2,1,0:T(8,128)(2,1)S(1)}, u32[]{:S(2)}, u32[]{:S(2)}) collective-permute-start(bf16[1,16,256]{2,1,0:T(8,128)(2,1)S(1)} %slice.198), channel_id=1, source_target_pairs={{8,0},{16,8},{24,16},{9,1},{17,9},{25,17},{10,2},{18,10},{26,18},{... | collective-permute-start | bytes 24584 | tf_op jit(solution)/shard_map/ppermute | solution.py:18
  19.9 13.0 %all-to-all-start = ((s32[1,8,2]{2,0,1:T(1,128)}), s32[1,8,2]{2,0,1:T(1,128)S(1)}, u32[]{:S(2)}, u32[]{:S(2)}) async-start(s32[1,8,2]{2,0,1:T(1,128)} %bitcast.75), calls=%async_computation | async-start | bytes 8192 | tf_op jit(solution)/shard_map/all_to_all | solution.py:133
  27.8 10.5 %copy-start.1 = (bf16[1,512,256]{2,1,0:T(8,128)(2,1)S(1)}, bf16[1,512,256]{2,1,0:T(8,128)(2,1)}, u32[]{:S(2)}) copy-start(bf16[1,512,256]{2,1,0:T(8,128)(2,1)} %param.8) | copy-start | bytes 786436
  33.0 23.1 %all-to-all-start.1 = ((bf16[1,8,2,128]{3,2,0,1:T(2,128)(2,1)}), bf16[1,8,2,128]{3,2,0,1:T(2,128)(2,1)S(1)}, u32[]{:S(2)}, u32[]{:S(2)}) async-start(bf16[1,8,2,128]{3,2,0,1:T(2,128)(2,1)} %fusion.162), calls=%async_computation.1 | async-start | bytes 8192 | tf_op jit(solution)/shard_map/all_to_all | solution.py:132
  37.0 188.6 %all-reduce.3.cloned.1.call-start = ((), (), s32[]{:S(2)}) async-start(), calls=%async_computation.2 | async-start | bytes 6291456 | tf_op jit(solution)/shard_map/psum | solution.py:118
  40.1 4.6 %collective-permute-start.1 = (bf16[1,4,256]{2,1,0:T(4,128)(2,1)S(1)}, bf16[1,4,256]{2,1,0:T(4,128)(2,1)S(1)}, u32[]{:S(2)}, u32[]{:S(2)}) collective-permute-start(bf16[1,4,256]{2,1,0:T(4,128)(2,1)S(1)} %slice.223), channel_id=1, source_target_pairs={{0,8},{8,16},{16,24},{1,9},{9,17},{17,25},{2,10},{10,18},{18,26},{... | collective-permute-start | bytes 6152 | tf_op jit(solution)/shard_map/ppermute | solution.py:18
  47.8 5.6 %collective-permute-start.2 = (bf16[1,8,256]{2,1,0:T(8,128)(2,1)S(1)}, bf16[1,8,256]{2,1,0:T(8,128)(2,1)S(1)}, u32[]{:S(2)}, u32[]{:S(2)}) collective-permute-start(bf16[1,8,256]{2,1,0:T(8,128)(2,1)S(1)} %slice.226), channel_id=1, source_target_pairs={{0,8},{8,16},{16,24},{1,9},{9,17},{17,25},{2,10},{10,18},{18,26},{... | collective-permute-start | bytes 12296 | tf_op jit(solution)/shard_map/ppermute | solution.py:18
  60.5 1.4 copy-start.3
  62.8 6.3 %collective-permute-start.4 = (bf16[1,8,256]{2,1,0:T(8,128)(2,1)S(1)}, bf16[1,8,256]{2,1,0:T(8,128)(2,1)S(1)}, u32[]{:S(2)}, u32[]{:S(2)}) collective-permute-start(bf16[1,8,256]{2,1,0:T(8,128)(2,1)S(1)} %slice.231), channel_id=1, source_target_pairs={{8,0},{16,8},{24,16},{9,1},{17,9},{25,17},{10,2},{18,10},{26,18},{... | collective-permute-start | bytes 12296 | tf_op jit(solution)/shard_map/ppermute | solution.py:18
  64.1 15.5 %collective-permute-start.7 = (bf16[1,16,256]{2,1,0:T(8,128)(2,1)S(1)}, bf16[1,16,256]{2,1,0:T(8,128)(2,1)S(1)}, u32[]{:S(2)}, u32[]{:S(2)}) collective-permute-start(bf16[1,16,256]{2,1,0:T(8,128)(2,1)S(1)} %slice.240), channel_id=1, source_target_pairs={{0,8},{8,16},{16,24},{1,9},{9,17},{17,25},{2,10},{10,18},{18,26},{... | collective-permute-start | bytes 24584 | tf_op jit(solution)/shard_map/ppermute | solution.py:18
  71.1 4.4 %collective-permute-start.5 = (bf16[1,4,256]{2,1,0:T(4,128)(2,1)S(1)}, bf16[1,4,256]{2,1,0:T(4,128)(2,1)S(1)}, u32[]{:S(2)}, u32[]{:S(2)}) collective-permute-start(bf16[1,4,256]{2,1,0:T(4,128)(2,1)S(1)} %slice.234), channel_id=1, source_target_pairs={{8,0},{16,8},{24,16},{9,1},{17,9},{25,17},{10,2},{18,10},{26,18},{... | collective-permute-start | bytes 6152 | tf_op jit(solution)/shard_map/ppermute | solution.py:18
  77.5 4.9 %collective-permute-start.6 = (bf16[1,2,256]{2,1,0:T(2,128)(2,1)S(1)}, bf16[1,2,256]{2,1,0:T(2,128)(2,1)S(1)}, u32[]{:S(2)}, u32[]{:S(2)}) collective-permute-start(bf16[1,2,256]{2,1,0:T(2,128)(2,1)S(1)} %slice.237), channel_id=1, source_target_pairs={{8,0},{16,8},{24,16},{9,1},{17,9},{25,17},{10,2},{18,10},{26,18},{... | collective-permute-start | bytes 3080 | tf_op jit(solution)/shard_map/ppermute | solution.py:18
Sparse Core Ops, SparseCore 0:
  82.4 143.1 all-reduce.2
where the time goes:
time: 237 us; the launch traced here: 236 us
  waiting for transfers between devices  98.4 us (42%)
  blocking collectives  44.3 us (19%)
  starting transfers between devices  30.8 us (13%)
  matrix products  24.5 us (10%)
  other arithmetic  17.1 us (7%)
  between operations  14.6 us (6%)
  local copies, waits for them, and re-layouts  6.56 us (3%)
    psum x1, waiting for transfers between devices, body(): lax.psum((weight_local, gain_local, bias_local), ('seq', 'user'))  93.8 us
    psum x1, blocking collectives, body(): lax.psum((weight_local, gain_local, bias_local), ('seq', 'user'))  44.3 us
    ppermute x8, starting transfers between devices, passed_along(): return lax.ppermute(block, axis, route)  20.1 us
    dot_general x9, matrix products, dilated(): jnp.dot(window, kernel[tap_index], preferred_element_type=jnp.float32)  10.6 us
    dot_general x12, matrix products, body(): lax.dot_general(window, weights[layer_num, tap_index], (((1,), (1,)), (()...  9.9 us
    all_to_all x1, starting transfers between devices, body(): lax.all_to_all(send_ids, 'user', split_axis=1, concat_axis=0, tiled=True)  6.62 us
  transfers between devices with their start and end apart: 11, of which 4 were waited for; matrix products, arithmetic and copies ran while one was open for 14% of the time, Pallas kernels for 0%

commit v1 on v0

v1 whole, which is shorter than its diff:
```python
import functools
import math

import jax
import jax.numpy as jnp
from jax import lax
from jax.experimental import pallas as pl
from jax.experimental.pallas import tpu as pltpu
from jax.sharding import PartitionSpec as P

TAPS = 3
LAYERS = 4
HALO = 32
CHUNK = 64
TAIL = 16
EPS = 1e-05
CURVE = math.sqrt(2.0 / math.pi)
CUBIC = 0.044715
MESH = pl.DeviceIdType.MESH
F32 = jnp.float32
BF16 = jnp.bfloat16


def table_blocks(pooled_ref, owner_ref, ids_ref, blocks_ref, per_owner):
    tables = pooled_ref.shape[0]
    owner_row = owner_ref[...].astype(F32)
    ids_row = ids_ref[...].astype(F32)
    first = lax.broadcasted_iota(jnp.int32, (tables, tables), 0)
    second = lax.broadcasted_iota(jnp.int32, (tables, tables), 1)
    owner_col = jnp.sum(jnp.where(first == second, owner_row, 0.0), 1, keepdims=True)
    ahead = (owner_col < owner_row) | ((owner_col == owner_row) & (first < second))
    rank_row = jnp.sum(jnp.where(ahead, 1.0, 0.0), 0, keepdims=True)
    picks = rank_row == first.astype(F32)
    rows = jnp.dot(
        jnp.where(picks, 1.0, 0.0).astype(BF16), pooled_ref[...], preferred_element_type=F32
    )
    ids = jnp.sum(jnp.where(picks, ids_row, 0.0), 1, keepdims=True)
    ids = jnp.broadcast_to(ids, rows.shape)
    blocks_ref[...] = jnp.zeros_like(blocks_ref)
    for user in range(blocks_ref.shape[0]):
        at = user * per_owner
        blocks_ref[user, 0:per_owner, :] = rows[at : at + per_owner]
        blocks_ref[user, per_owner : 2 * per_owner, :] = ids[at : at + per_owner]


def fold(values):
    return jnp.sum(values.reshape(values.shape[0] // 8, 8, values.shape[1]), 0)


def stack_kernel(
    per_owner,
    hist_ref, left_ref, right_ref, cot_ref, weights_ref, gain_ref, bias_ref,
    pooled_ref, owner_ref, ids_ref,
    dhist_ref, part_ref, small_ref, blocks_ref,
    x_ref, normed_ref, rstd_ref, act_ref, shifted_ref, flow_ref, ahead_ref, back_ref,
):
    length, channels = hist_ref.shape
    total = length + 2 * HALO
    seq = lax.axis_index("seq")
    oldest = jnp.where(seq == 0, HALO, 0)
    newest = jnp.where(seq == lax.axis_size("seq") - 1, 0.0, 1.0).astype(F32)

    table_blocks(pooled_ref, owner_ref, ids_ref, blocks_ref, per_owner)

    x_ref[0:HALO, :] = left_ref[...].astype(F32)
    x_ref[HALO : HALO + length, :] = hist_ref[...].astype(F32)
    x_ref[HALO + length : total, :] = right_ref[0:HALO, :].astype(F32)

    for layer in range(LAYERS):
        dilation = 2**layer
        gain = gain_ref[layer : layer + 1, :]

        def forward(step, tail, layer=layer, dilation=dilation, gain=gain):
            start = pl.multiple_of(step * CHUNK, CHUNK)
            rows = pl.ds(start, CHUNK)
            x = x_ref[rows, :]
            center = x - jnp.mean(x, -1, keepdims=True)
            rstd = lax.rsqrt(jnp.mean(center * center, -1, keepdims=True) + EPS)
            normed = center * rstd
            normed_ref[layer, rows, :] = normed
            rstd_ref[layer, rows, :] = jnp.broadcast_to(rstd, (CHUNK, 128))
            a = normed * gain
            act = 0.5 * a * (1.0 + jnp.tanh(CURVE * (a + CUBIC * (a * a * a))))
            where = start + lax.broadcasted_iota(jnp.int32, act.shape, 0)
            act = jnp.where(where >= oldest, act, 0.0)
            act_ref[layer, rows, :] = act.astype(BF16)
            window = jnp.concatenate([tail, act], 0)
            for tap in range(TAPS):
                offset = TAIL - tap * dilation
                shifted_ref[rows, tap * channels : (tap + 1) * channels] = window[
                    offset : offset + CHUNK
                ].astype(BF16)
            return act[CHUNK - TAIL :]

        lax.fori_loop(0, total // CHUNK, forward, jnp.zeros((TAIL, channels), F32))
        if layer < LAYERS - 1:
            x_ref[...] = (
                x_ref[...]
                + bias_ref[layer : layer + 1, :]
                + jnp.dot(shifted_ref[...], weights_ref[layer], preferred_element_type=F32)
            )

    def put_flow(rows, size, flow, head, dilation):
        flow_ref[rows, :] = flow
        if dilation is None:
            return
        window = jnp.concatenate([flow, head], 0)
        for tap in range(TAPS):
            offset = tap * dilation
            ahead_ref[rows, tap * channels : (tap + 1) * channels] = window[
                offset : offset + size
            ].astype(BF16)

    chunks = length // CHUNK
    zero_head = jnp.zeros((TAIL, channels), F32)
    zero_sum = jnp.zeros((8, channels), F32)

    future = right_ref[HALO : 2 * HALO, :].astype(F32) * newest
    put_flow(pl.ds(length, HALO), HALO, future, zero_head, 2 ** (LAYERS - 1))

    def begin(step, carry):
        head, bias_sum = carry
        rows = pl.ds(pl.multiple_of((chunks - 1 - step) * CHUNK, CHUNK), CHUNK)
        flow = cot_ref[rows, :].astype(F32)
        put_flow(rows, CHUNK, flow, head, 2 ** (LAYERS - 1))
        return flow[:TAIL], bias_sum + fold(flow)

    _, bias_sum = lax.fori_loop(0, chunks, begin, (future[:TAIL], zero_sum))

    for layer in reversed(range(LAYERS)):
        small_ref[1, layer : layer + 1, :] = jnp.sum(bias_sum, 0, keepdims=True)
        grads = lax.dot_general(
            act_ref[layer, HALO : HALO + length, :],
            ahead_ref[0:length, :],
            (((0,), (0,)), ((), ())),
            preferred_element_type=F32,
        )
        for tap in range(TAPS):
            for half in range(2):
                at = tap * channels + half * (channels // 2)
                part_ref[layer, half, tap * channels : (tap + 1) * channels, :] = grads[
                    :, at : at + channels // 2
                ].astype(BF16)
        back = None
        for tap in range(TAPS):
            one = lax.dot_general(
                ahead_ref[:, tap * channels : (tap + 1) * channels],
                weights_ref[layer, tap * channels : (tap + 1) * channels, :],
                (((1,), (1,)), ((), ())),
                preferred_element_type=F32,
            )
            back = one if back is None else back + one
        back_ref[...] = back
        gain = gain_ref[layer : layer + 1, :]
        below = 2 ** (layer - 1) if layer else None

        def through(start, size, layer=layer, gain=gain):
            rows = pl.ds(start, size)
            held = pl.ds(start + HALO, size)
            normed = normed_ref[layer, held, :]
            rstd = rstd_ref[layer, held, :][:, 0:1]
            a = normed * gain
            squared = a * a
            t = jnp.tanh(CURVE * (a + CUBIC * (squared * a)))
            slope = 0.5 * (1.0 + t) + 0.5 * a * (1.0 - t * t) * (
                CURVE * (1.0 + 3.0 * CUBIC * squared)
            )
            pre = slope * back_ref[rows, :]
            taken = pre * normed
            q = pre * gain
            mean_q = jnp.mean(q, -1, keepdims=True)
            mean_qn = jnp.mean(q * normed, -1, keepdims=True)
            flow = flow_ref[rows, :] + rstd * (q - mean_q - normed * mean_qn)
            return flow, taken

        if layer:
            future, _ = through(length, HALO)
            future = future * newest
            put_flow(pl.ds(length, HALO), HALO, future, zero_head, below)
        else:
            future = zero_head

        def backward(step, carry, layer=layer, below=below, through=through):
            head, bias_sum, gain_sum = carry
            start = pl.multiple_of((chunks - 1 - step) * CHUNK, CHUNK)
            rows = pl.ds(start, CHUNK)
            flow, taken = through(start, CHUNK)
            if layer:
                put_flow(rows, CHUNK, flow, head, below)
            else:
                dhist_ref[rows, :] = flow.astype(BF16)
            return flow[:TAIL], bias_sum + fold(flow), gain_sum + fold(taken)

        _, bias_sum, gain_sum = lax.fori_loop(
            0, chunks, backward, (future[:TAIL], zero_sum, zero_sum)
        )
        small_ref[0, layer : layer + 1, :] = jnp.sum(gain_sum, 0, keepdims=True)


def sum_kernel(
    per_owner,
    part_ref, small_ref, blocks_ref,
    out_ref, total_ref, table_ref,
    core_recv, y_send, y_recv, u_send, u_recv, final,
    small_core, small_y_send, small_y, small_u_send, small_u, rows_in,
    sems_out, sems_in,
):
    layers, _, ys, users = part_ref.shape[:4]
    seq, user = lax.axis_index("seq"), lax.axis_index("user")
    y, core = seq // 2, seq % 2
    sibling = {"seq": y * 2 + 1 - core, "user": user}

    def of_y(step):
        other = lax.rem(y + step, ys)
        return other, {"seq": other * 2 + core, "user": user}

    def of_user(step):
        other = lax.rem(user + step, users)
        return other, {"seq": seq, "user": other}

    barrier = pltpu.get_barrier_semaphore()
    partners = [sibling] + [of_y(s)[1] for s in range(1, ys)]
    partners += [of_user(s)[1] for s in range(1, users)]
    for partner in partners:
        pl.semaphore_signal(barrier, inc=1, device_id=partner, device_id_type=MESH)
    pl.semaphore_wait(barrier, len(partners))

    used = [0]

    def send(src, dst, device):
        slot = used[0]
        used[0] += 1
        copy = pltpu.make_async_remote_copy(
            src_ref=src,
            dst_ref=dst,
            send_sem=sems_out.at[slot],
            recv_sem=sems_in.at[slot],
            device_id=device,
            device_id_type=MESH,
        )
        copy.start()
        return copy

    core_copies = [send(part_ref.at[:, 1 - core], core_recv, sibling)]
    core_copies.append(send(small_ref, small_core, sibling))
    table_copies = []
    for step in range(1, users):
        other, device = of_user(step)
        table_copies.append(send(blocks_ref.at[other], rows_in.at[user], device))
    for copy in core_copies:
        copy.wait()

    for layer in range(layers):
        y_send[layer] = (
            part_ref[layer, core].astype(F32) + core_recv[layer].astype(F32)
        ).astype(BF16)
    small_y_send[...] = small_ref[...] + small_core[...]
    y_copies = []
    for step in range(1, ys):
        other, device = of_y(step)
        y_copies.append(send(y_send.at[:, other], y_recv.at[:, step - 1], device))
        y_copies.append(send(small_y_send, small_y.at[y], device))
    small_y[y] = small_y_send[...]
    for copy in y_copies:
        copy.wait()
    for layer in range(layers):
        summed = y_send[layer, y].astype(F32)
        for step in range(1, ys):
            summed = summed + y_recv[layer, step - 1].astype(F32)
        u_send[layer] = summed.astype(BF16)
    small_sum = small_y[0]
    for other in range(1, ys):
        small_sum = small_sum + small_y[other]
    small_u_send[...] = small_sum

    u_copies = []
    for step in range(1, users):
        other, device = of_user(step)
        u_copies.append(send(u_send.at[:, other], u_recv.at[:, step - 1], device))
        u_copies.append(send(small_u_send, small_u.at[user], device))
    small_u[user] = small_u_send[...]
    rows_in[user] = blocks_ref[user]
    for copy in table_copies:
        copy.wait()
    for table in range(per_owner):
        ids = rows_in[:, per_owner + table, :]
        found = jnp.zeros(ids.shape, F32)
        for other in range(users):
            match = ids == ids[other : other + 1, :]
            found = found + jnp.where(match, rows_in[other, table : table + 1, :], 0.0)
        table_ref[table] = found
    for copy in u_copies:
        copy.wait()
    for layer in range(layers):
        summed = u_send[layer, user].astype(F32)
        for step in range(1, users):
            summed = summed + u_recv[layer, step - 1].astype(F32)
        final[layer, core, y, user] = summed.astype(BF16)

    spread = []
    for step in range(1, users):
        _, device = of_user(step)
        mine = final.at[:, core, y, user]
        spread.append(send(mine, mine, device))
    small_sum = small_u[0]
    for other in range(1, users):
        small_sum = small_sum + small_u[other]
    total_ref[...] = small_sum
    for copy in spread:
        copy.wait()
    spread = []
    for step in range(1, ys):
        _, device = of_y(step)
        mine = final.at[:, core, y]
        spread.append(send(mine, mine, device))
    for copy in spread:
        copy.wait()
    mine = final.at[:, core]
    send(mine, mine, sibling).wait()
    out_ref[...] = final[...]


def passed_along(block, distance):
    devices = range(lax.axis_size("seq"))
    route = [(i - distance, i) for i in devices if i - distance in devices]
    return lax.ppermute(block, "seq", route)


def body(history, cotangent, weights, ln_gain, conv_bias, pooled_grad, table_owner, row_ids):
    _, length, channels = history.shape
    users, seqs = lax.axis_size("user"), lax.axis_size("seq")
    ys = seqs // 2
    tables = table_owner.shape[0]
    per_owner = tables // users
    lanes = pooled_grad.shape[2]
    block_rows = max(8, 2 * per_owner)
    piece = TAPS * channels // (ys * users)
    history, cotangent = history[0], cotangent[0]
    left = passed_along(history[length - HALO :], 1)
    right = passed_along(jnp.concatenate([history[:HALO], cotangent[:HALO]], 0), -1)
    total = length + 2 * HALO
    vmem = pl.BlockSpec(memory_space=pltpu.VMEM)
    half = channels // 2

    d_history, part, small, blocks = pl.pallas_call(
        functools.partial(stack_kernel, per_owner),
        out_shape=(
            jax.ShapeDtypeStruct((length, channels), BF16),
            jax.ShapeDtypeStruct((LAYERS, 2, TAPS * channels, half), BF16),
            jax.ShapeDtypeStruct((2, LAYERS, channels), F32),
            jax.ShapeDtypeStruct((users, block_rows, lanes), F32),
        ),
        in_specs=[vmem] * 10,
        out_specs=(vmem,) * 4,
        scratch_shapes=[
            pltpu.VMEM((total, channels), F32),
            pltpu.VMEM((LAYERS, total, channels), F32),
            pltpu.VMEM((LAYERS, total, 128), F32),
            pltpu.VMEM((LAYERS, total, channels), BF16),
            pltpu.VMEM((total, TAPS * channels), BF16),
            pltpu.VMEM((length + HALO, channels), F32),
            pltpu.VMEM((length + HALO, TAPS * channels), BF16),
            pltpu.VMEM((length + HALO, channels), F32),
        ],
        compiler_params=pltpu.CompilerParams(vmem_limit_bytes=48 << 20),
        name="stack",
    )(
        history, left, right, cotangent,
        weights.reshape(LAYERS, TAPS * channels, channels), ln_gain, conv_bias,
        pooled_grad[0], table_owner.reshape(1, tables), row_ids,
    )

    part = part.reshape(LAYERS, 2, ys, users, piece, half)
    copies = 3 + 4 * (users - 1) + 3 * (ys - 1)
    grid = (ys, users, piece, half)
    sums, total_small, table_grad = pl.pallas_call(
        functools.partial(sum_kernel, per_owner),
        out_shape=(
            jax.ShapeDtypeStruct((LAYERS, 2) + grid, BF16),
            jax.ShapeDtypeStruct((2, LAYERS, channels), F32),
            jax.ShapeDtypeStruct((per_owner, users, lanes), F32),
        ),
        in_specs=[vmem] * 3,
        out_specs=(vmem,) * 3,
        scratch_shapes=[
            pltpu.VMEM((LAYERS,) + grid, BF16),
            pltpu.VMEM((LAYERS,) + grid, BF16),
            pltpu.VMEM((LAYERS, max(ys - 1, 1), users, piece, half), BF16),
            pltpu.VMEM((LAYERS, users, piece, half), BF16),
            pltpu.VMEM((LAYERS, users - 1, piece, half), BF16),
            pltpu.VMEM((LAYERS, 2) + grid, BF16),
            pltpu.VMEM((2, LAYERS, channels), F32),
            pltpu.VMEM((2, LAYERS, channels), F32),
            pltpu.VMEM((ys, 2, LAYERS, channels), F32),
            pltpu.VMEM((2, LAYERS, channels), F32),
            pltpu.VMEM((users, 2, LAYERS, channels), F32),
            pltpu.VMEM((users, block_rows, lanes), F32),
            pltpu.SemaphoreType.DMA((copies,)),
            pltpu.SemaphoreType.DMA((copies,)),
        ],
        compiler_params=pltpu.CompilerParams(
            collective_id=0, has_side_effects=True, vmem_limit_bytes=48 << 20
        ),
        name="sums",
    )(part, small, blocks)

    factor = 1.0 / math.sqrt(users * length * seqs)
    sums = sums.reshape(LAYERS, 2, TAPS, channels, half).astype(F32) * factor
    grad_weights = jnp.concatenate([sums[:, 0], sums[:, 1]], -1)
    total_small = total_small * factor
    return d_history[None], grad_weights, total_small[0], total_small[1], table_grad


def solution(mesh):
    in_specs = (
        P("user", "seq", None),
        P("user", "seq", None),
        P(),
        P(),
        P(),
        P("user", "seq", None),
        P("seq"),
        P("user", "seq"),
    )
    out_specs = (P("user", "seq", None), P(), P(), P(), P(("seq", "user"), None, None))
    return jax.shard_map(body, mesh=mesh, in_specs=in_specs, out_specs=out_specs, check_vma=False)
```

time: 237 us -> 90.3 us (0.38)
  the two profiles are of different devices: /device:TPU:0 before, /device:TPU:31 now
where the time goes in v1:
time: 90.3 us; the launch traced here: 89.8 us
  Pallas kernels  72.3 us (80%)
  local copies, waits for them, and re-layouts  8.94 us (10%)
  starting transfers between devices  3.86 us (4%)
  other arithmetic  2.2 us (2%)
  waiting for transfers between devices  1.78 us (2%)
    pallas_call x1, Pallas kernels, body(): pl.pallas_call(functools.partial(sum_kernel, per_owner), out_shape=(jax.S...  52.7 us
    pallas_call x1, Pallas kernels, body(): pl.pallas_call(functools.partial(stack_kernel, per_owner), out_shape=(jax...  19.7 us
    unnamed x17, local copies, waits for them, and re-layouts  7.27 us
    ppermute x2, starting transfers between devices, passed_along(): return lax.ppermute(block, 'seq', route)  3.86 us
    concatenate x1, other arithmetic, body(): grad_weights = jnp.concatenate([sums[:, 0], sums[:, 1]], -1)  1.9 us
  transfers between devices with their start and end apart: 2, of which 1 were waited for; matrix products, arithmetic and copies ran while one was open for 0% of the time, Pallas kernels for 0%

profile of v1, /device:TPU:31, one launch (start us, length us, event | category | flops | bytes accessed | tf_op | source)
XLA Modules:
  0.0 89.8 jit_solution(10235112490553879776)
XLA Ops:
  0.6 0.8 slice_bitcast_fusion.3
  1.4 2.6 %collective-permute-start.1 = (bf16[64,256]{1,0:T(8,128)(2,1)S(1)}, bf16[64,256]{1,0:T(8,128)(2,1)S(1)}, u32[]{:S(2)}, u32[]{:S(2)}) collective-permute-start(bf16[64,256]{1,0:T(8,128)(2,1)S(1)} %pad_maximum_fusion.1), channel_id=1, source_target_pairs={{8,0},{16,8},{24,16},{9,1},{17,9},{25,17},{10,2},{18,10},{26,18},{... | collective-permute-start | bytes 98312 | tf_op jit(solution)/shard_map/ppermute | solution.py:326
  4.0 1.3 %collective-permute-start = (bf16[32,256]{1,0:T(8,128)(2,1)S(1)}, bf16[32,256]{1,0:T(8,128)(2,1)S(1)}, u32[]{:S(2)}, u32[]{:S(2)}) collective-permute-start(bf16[32,256]{1,0:T(8,128)(2,1)S(1)} %get-tuple-element.22), channel_id=1, source_target_pairs={{0,8},{8,16},{16,24},{1,9},{9,17},{17,25},{2,10},{10,18},{18,26},{... | collective-permute-start | bytes 49160 | tf_op jit(solution)/shard_map/ppermute | solution.py:326
  5.3 1.8 %collective-permute-done.left_ref = bf16[32,256]{1,0:T(8,128)(2,1)S(1)} collective-permute-done((bf16[32,256]{1,0:T(8,128)(2,1)S(1)}, bf16[32,256]{1,0:T(8,128)(2,1)S(1)}, u32[]{:S(2)}, u32[]{:S(2)}) %collective-permute-start) | collective-permute-done | bytes 16416 | tf_op jit(solution)/shard_map/ppermute | solution.py:326
  7.1 0.0 collective-permute-done.1.right_ref
  7.1 0.0 copy-start
  7.1 1.4 %copy-done = bf16[4,3,256,256]{3,2,1,0:T(8,128)(2,1)S(1)} copy-done((bf16[4,3,256,256]{3,2,1,0:T(8,128)(2,1)S(1)}, bf16[4,3,256,256]{3,2,1,0:T(8,128)(2,1)}, u32[]{:S(2)}) %copy-start) | copy-done | bytes 1572888
  8.5 0.0 copy-start.1
  8.5 0.9 %copy-done.1 = bf16[1,512,256]{2,1,0:T(8,128)(2,1)S(1)} copy-done((bf16[1,512,256]{2,1,0:T(8,128)(2,1)S(1)}, bf16[1,512,256]{2,1,0:T(8,128)(2,1)}, u32[]{:S(2)}) %copy-start.1) | copy-done | bytes 262168
  9.4 0.0 copy-start.2
  9.4 0.9 %copy-done.2 = bf16[1,512,256]{2,1,0:T(8,128)(2,1)S(1)} copy-done((bf16[1,512,256]{2,1,0:T(8,128)(2,1)S(1)}, bf16[1,512,256]{2,1,0:T(8,128)(2,1)}, u32[]{:S(2)}) %copy-start.2) | copy-done | bytes 262168
  10.4 0.0 copy-start.3
  10.4 0.7 copy-done.3
  11.1 0.0 copy-start.4
  11.1 0.7 copy-done.4
  11.7 0.0 copy-start.5
  11.7 0.7 copy-done.5
  12.4 0.0 copy-start.6
  12.4 0.7 copy-done.6
  13.1 0.0 copy-start.7
  13.1 0.7 copy-done.7
  13.7 19.7 %stack.1 = (bf16[512,256]{1,0:T(8,128)(2,1)}, bf16[4,2,768,128]{3,2,1,0:T(8,128)(2,1)S(1)}, f32[2,4,256]{2,1,0:T(4,128)S(1)}, f32[8,8,128]{2,1,0:T(8,128)S(1)}) custom-call(bf16[512,256]{1,0:T(8,128)(2,1)S(1)} %bitcast.28, bf16[32,256]{1,0:T(8,128)(2,1)S(1)} %collective-permute-done.left_ref, bf16[64,256]{1,0:T(8,128)(2,1)S(1)} %collective-permute-done.1.right_ref, ...), custom_call_target="tpu_custom_call" | custom-call | tf_op jit(solution)/shard_map/stack/pallas_call | solution.py:345
  33.4 52.7 %sums.1 = (bf16[4,2,2,8,48,128]{5,4,3,2,1,0:T(8,128)(2,1)S(1)}, f32[2,4,256]{2,1,0:T(4,128)S(1)}, f32[2,8,128]{2,1,0:T(8,128)S(1)}) custom-call(bf16[4,2,2,8,48,128]{5,4,3,2,1,0:T(8,128)(2,1)S(1)} %bitcast.26, f32[2,4,256]{2,1,0:T(4,128)S(1)} %get-tuple-element.14.small_ref, f32[8,8,128]{2,1,0:T(8,128)S(1)} %get-tuple-element.15.blocks_ref), custom_call_target="tpu_custom_call" | custom-call | tf_op jit(solution)/shard_map/sums/pallas_call | solution.py:376
  86.1 0.6 slice_bitcast_fusion.5
  86.7 0.3 convert_multiply_fusion
  87.0 0.3 slice_bitcast_fusion.1
  87.3 1.9 %pad_maximum_fusion = f32[4,3,256,256]{3,2,1,0:T(8,128)} fusion(f32[4,3,256,128]{3,2,1,0:T(8,128)S(1)} %get-tuple-element.20, f32[4,3,256,128]{3,2,1,0:T(8,128)S(1)} %get-tuple-element.19), kind=kLoop, calls=%fused_computation | loop fusion | flops 786432 | bytes 6291456 | tf_op jit(solution)/shard_map/concatenate | solution.py:409
  89.2 0.6 copy.18
  (2 shorter events, 0.0 us)
Async XLA Ops:
  1.4 5.7 %collective-permute-start.1 = (bf16[64,256]{1,0:T(8,128)(2,1)S(1)}, bf16[64,256]{1,0:T(8,128)(2,1)S(1)}, u32[]{:S(2)}, u32[]{:S(2)}) collective-permute-start(bf16[64,256]{1,0:T(8,128)(2,1)S(1)} %pad_maximum_fusion.1), channel_id=1, source_target_pairs={{8,0},{16,8},{24,16},{9,1},{17,9},{25,17},{10,2},{18,10},{26,18},{... | collective-permute-start | bytes 98312 | tf_op jit(solution)/shard_map/ppermute | solution.py:326
  4.0 3.1 %collective-permute-start = (bf16[32,256]{1,0:T(8,128)(2,1)S(1)}, bf16[32,256]{1,0:T(8,128)(2,1)S(1)}, u32[]{:S(2)}, u32[]{:S(2)}) collective-permute-start(bf16[32,256]{1,0:T(8,128)(2,1)S(1)} %get-tuple-element.22), channel_id=1, source_target_pairs={{0,8},{8,16},{16,24},{1,9},{9,17},{17,25},{2,10},{10,18},{18,26},{... | collective-permute-start | bytes 49160 | tf_op jit(solution)/shard_map/ppermute | solution.py:326
  7.1 1.4 %copy-start = (bf16[4,3,256,256]{3,2,1,0:T(8,128)(2,1)S(1)}, bf16[4,3,256,256]{3,2,1,0:T(8,128)(2,1)}, u32[]{:S(2)}) copy-start(bf16[4,3,256,256]{3,2,1,0:T(8,128)(2,1)} %param.10) | copy-start | bytes 4718596
  8.5 0.9 %copy-start.1 = (bf16[1,512,256]{2,1,0:T(8,128)(2,1)S(1)}, bf16[1,512,256]{2,1,0:T(8,128)(2,1)}, u32[]{:S(2)}) copy-start(bf16[1,512,256]{2,1,0:T(8,128)(2,1)} %param.8) | copy-start | bytes 786436
  9.4 0.9 %copy-start.2 = (bf16[1,512,256]{2,1,0:T(8,128)(2,1)S(1)}, bf16[1,512,256]{2,1,0:T(8,128)(2,1)}, u32[]{:S(2)}) copy-start(bf16[1,512,256]{2,1,0:T(8,128)(2,1)} %param.9) | copy-start | bytes 786436
  10.4 0.7 copy-start.3
  11.1 0.7 copy-start.4
  11.7 0.7 copy-start.5
  12.4 0.7 copy-start.6
  13.1 0.7 copy-start.7

commit v2 on v1

v2 whole, which is shorter than its diff:
```python
import functools
import math

import jax
import jax.numpy as jnp
from jax import lax
from jax.experimental import pallas as pl
from jax.experimental.pallas import tpu as pltpu
from jax.sharding import PartitionSpec as P

TAPS = 3
LAYERS = 4
HALO = 32
CHUNK = 64
TAIL = 16
EPS = 1e-05
CURVE = math.sqrt(2.0 / math.pi)
CUBIC = 0.044715
MESH = pl.DeviceIdType.MESH
F32 = jnp.float32
BF16 = jnp.bfloat16


def table_blocks(pooled_ref, owner_ref, ids_ref, blocks_ref, per_owner):
    tables = pooled_ref.shape[0]
    owner_row = owner_ref[...].astype(F32)
    ids_row = ids_ref[...].astype(F32)
    first = lax.broadcasted_iota(jnp.int32, (tables, tables), 0)
    second = lax.broadcasted_iota(jnp.int32, (tables, tables), 1)
    owner_col = jnp.sum(jnp.where(first == second, owner_row, 0.0), 1, keepdims=True)
    ahead = (owner_col < owner_row) | ((owner_col == owner_row) & (first < second))
    rank_row = jnp.sum(jnp.where(ahead, 1.0, 0.0), 0, keepdims=True)
    picks = rank_row == first.astype(F32)
    rows = jnp.dot(
        jnp.where(picks, 1.0, 0.0).astype(BF16), pooled_ref[...], preferred_element_type=F32
    )
    ids = jnp.sum(jnp.where(picks, ids_row, 0.0), 1, keepdims=True)
    ids = jnp.broadcast_to(ids, rows.shape)
    blocks_ref[...] = jnp.zeros_like(blocks_ref)
    for user in range(blocks_ref.shape[0]):
        at = user * per_owner
        blocks_ref[user, 0:per_owner, :] = rows[at : at + per_owner]
        blocks_ref[user, per_owner : 2 * per_owner, :] = ids[at : at + per_owner]


def fold(values):
    return jnp.sum(values.reshape(values.shape[0] // 8, 8, values.shape[1]), 0)


def step_kernel(
    per_owner,
    hist_hbm, cot_hbm, weights_hbm, gain_hbm, bias_hbm, pooled_hbm, owner_hbm, ids_hbm,
    dhist_ref, out_ref, total_ref, table_ref,
    hist_ref, cot_ref, weights_ref, gain_ref, bias_ref, pooled_ref, owner_ref, ids_ref,
    left_ref, right_ref,
    x_ref, normed_ref, rstd_ref, act_ref, shifted_ref, flow_ref, ahead_ref, back_ref,
    part_ref, core_recv, y_send, y_recv, u_send, u_recv, final,
    small_ref, small_core, small_y_send, small_y, small_u_send, small_u,
    blocks_ref, rows_in,
    sems_local, sems_out, sems_in,
):
    length, channels = hist_ref.shape
    total = length + 2 * HALO
    users, seqs = lax.axis_size("user"), lax.axis_size("seq")
    ys = seqs // 2
    half = channels // 2
    rows_all = part_ref.shape[2]
    piece = rows_all // (ys * users)
    seq, user = lax.axis_index("seq"), lax.axis_index("user")
    y, core = seq // 2, seq % 2
    sibling = {"seq": y * 2 + 1 - core, "user": user}
    oldest = jnp.where(seq == 0, HALO, 0)
    newest = jnp.where(seq == seqs - 1, 0.0, 1.0).astype(F32)

    local = []
    pairs = (
        (pooled_hbm, pooled_ref), (owner_hbm, owner_ref), (ids_hbm, ids_ref),
        (hist_hbm, hist_ref), (gain_hbm, gain_ref), (bias_hbm, bias_ref),
        (weights_hbm, weights_ref), (cot_hbm, cot_ref),
    )
    for slot, (src, dst) in enumerate(pairs):
        copy = pltpu.make_async_copy(src, dst, sems_local.at[slot])
        copy.start()
        local.append(copy)

    def of_seq(step):
        return {"seq": lax.rem(seq + step, seqs), "user": user}

    def of_y(step):
        other = lax.rem(y + step, ys)
        return other, {"seq": other * 2 + core, "user": user}

    def of_user(step):
        other = lax.rem(user + step, users)
        return other, {"seq": seq, "user": other}

    barrier = pltpu.get_barrier_semaphore()
    for step in range(1, seqs):
        pl.semaphore_signal(barrier, inc=1, device_id=of_seq(step), device_id_type=MESH)
    for step in range(1, users):
        pl.semaphore_signal(barrier, inc=1, device_id=of_user(step)[1], device_id_type=MESH)
    pl.semaphore_wait(barrier, seqs + users - 2)

    used = [0]

    def send(src, dst, device):
        slot = used[0]
        used[0] += 1
        copy = pltpu.make_async_remote_copy(
            src_ref=src,
            dst_ref=dst,
            send_sem=sems_out.at[slot],
            recv_sem=sems_in.at[slot],
            device_id=device,
            device_id_type=MESH,
        )
        copy.start()
        return copy

    halo = [
        send(hist_hbm.at[length - HALO : length], left_ref, of_seq(1)),
        send(hist_hbm.at[0:HALO], right_ref.at[0:HALO], of_seq(seqs - 1)),
        send(cot_hbm.at[0:HALO], right_ref.at[HALO : 2 * HALO], of_seq(seqs - 1)),
    ]

    for copy in local[:3]:
        copy.wait()
    table_blocks(pooled_ref, owner_ref, ids_ref, blocks_ref, per_owner)
    for copy in local[3:]:
        copy.wait()
    for copy in halo:
        copy.wait()
    table_copies = []
    for step in range(1, users):
        other, device = of_user(step)
        table_copies.append(send(blocks_ref.at[other], rows_in.at[user], device))

    def piece_rows(y_index, user_index):
        return pl.ds(pl.multiple_of((y_index * users + user_index) * piece, 16), piece)

    def y_rows(y_index):
        return pl.ds(pl.multiple_of(y_index * (users * piece), 16), users * piece)

    def user_rows(user_index):
        return pl.ds(pl.multiple_of(user_index * piece, 16), piece)

    def add(first, others):
        summed = first.astype(F32)
        for other in others:
            summed = summed + other.astype(F32)
        return summed.astype(BF16)

    def course(layer):
        flying = [send(part_ref.at[layer, 1 - core], core_recv.at[layer], sibling)]
        yield
        for copy in flying:
            copy.wait()
        y_send[layer] = add(part_ref[layer, core], [core_recv[layer]])
        flying = []
        for step in range(1, ys):
            other, device = of_y(step)
            flying.append(send(y_send.at[layer, y_rows(other)], y_recv.at[layer, step - 1], device))
        yield
        for copy in flying:
            copy.wait()
        u_send[layer] = add(
            y_send[layer, y_rows(y), :], [y_recv[layer, step] for step in range(ys - 1)]
        )
        flying = []
        for step in range(1, users):
            other, device = of_user(step)
            flying.append(
                send(u_send.at[layer, user_rows(other)], u_recv.at[layer, step - 1], device)
            )
        yield
        for copy in flying:
            copy.wait()
        final[layer, core, piece_rows(y, user), :] = add(
            u_send[layer, user_rows(user), :], [u_recv[layer, step] for step in range(users - 1)]
        )
        mine = final.at[layer, core, piece_rows(y, user)]
        flying = [send(mine, mine, of_user(step)[1]) for step in range(1, users)]
        yield
        for copy in flying:
            copy.wait()
        mine = final.at[layer, core, y_rows(y)]
        flying = [send(mine, mine, of_y(step)[1]) for step in range(1, ys)]
        yield
        for copy in flying:
            copy.wait()
        mine = final.at[layer, core]
        flying = [send(mine, mine, sibling)]
        yield
        for copy in flying:
            copy.wait()
        out_ref[layer] = final[layer, :, 0 : TAPS * channels, :]

    def small_course():
        flying = [send(small_ref, small_core, sibling)]
        yield
        for copy in flying:
            copy.wait()
        small_y_send[...] = small_ref[...] + small_core[...]
        flying = [send(small_y_send, small_y.at[y], of_y(step)[1]) for step in range(1, ys)]
        small_y[y] = small_y_send[...]
        yield
        for copy in flying:
            copy.wait()
        small_sum = small_y[0]
        for other in range(1, ys):
            small_sum = small_sum + small_y[other]
        small_u_send[...] = small_sum
        flying = [send(small_u_send, small_u.at[user], of_user(step)[1]) for step in range(1, users)]
        small_u[user] = small_u_send[...]
        yield
        for copy in flying:
            copy.wait()
        small_sum = small_u[0]
        for other in range(1, users):
            small_sum = small_sum + small_u[other]
        total_ref[...] = small_sum

    def tables_course():
        rows_in[user] = blocks_ref[user]
        for copy in table_copies:
            copy.wait()
        for table in range(per_owner):
            ids = rows_in[:, per_owner + table, :]
            found = jnp.zeros(ids.shape, F32)
            for other in range(users):
                match = ids == ids[other : other + 1, :]
                found = found + jnp.where(match, rows_in[other, table : table + 1, :], 0.0)
            table_ref[table] = found
        return
        yield

    running = []

    def advance():
        for item in list(running):
            if next(item, "done") == "done":
                running.remove(item)

    def launch(item):
        if next(item, "done") != "done":
            running.append(item)

    if rows_all > TAPS * channels:
        part_ref[...] = jnp.zeros_like(part_ref)

    x_ref[0:HALO, :] = left_ref[...].astype(F32)
    x_ref[HALO : HALO + length, :] = hist_ref[...].astype(F32)
    x_ref[HALO + length : total, :] = right_ref[0:HALO, :].astype(F32)

    for layer in range(LAYERS):
        dilation = 2**layer
        gain = gain_ref[layer : layer + 1, :]

        def forward(step, tail, layer=layer, dilation=dilation, gain=gain):
            start = pl.multiple_of(step * CHUNK, CHUNK)
            rows = pl.ds(start, CHUNK)
            x = x_ref[rows, :]
            center = x - jnp.mean(x, -1, keepdims=True)
            rstd = lax.rsqrt(jnp.mean(center * center, -1, keepdims=True) + EPS)
            normed = center * rstd
            normed_ref[layer, rows, :] = normed
            rstd_ref[layer, rows, :] = jnp.broadcast_to(rstd, (CHUNK, 128))
            a = normed * gain
            act = 0.5 * a * (1.0 + jnp.tanh(CURVE * (a + CUBIC * (a * a * a))))
            where = start + lax.broadcasted_iota(jnp.int32, act.shape, 0)
            act = jnp.where(where >= oldest, act, 0.0)
            act_ref[layer, rows, :] = act.astype(BF16)
            window = jnp.concatenate([tail, act], 0)
            for tap in range(TAPS):
                offset = TAIL - tap * dilation
                shifted_ref[rows, tap * channels : (tap + 1) * channels] = window[
                    offset : offset + CHUNK
                ].astype(BF16)
            return act[CHUNK - TAIL :]

        lax.fori_loop(0, total // CHUNK, forward, jnp.zeros((TAIL, channels), F32))
        if layer < LAYERS - 1:
            x_ref[...] = (
                x_ref[...]
                + bias_ref[layer : layer + 1, :]
                + jnp.dot(shifted_ref[...], weights_ref[layer], preferred_element_type=F32)
            )

    def put_flow(rows, size, flow, head, dilation):
        flow_ref[rows, :] = flow
        if dilation is None:
            return
        window = jnp.concatenate([flow, head], 0)
        for tap in range(TAPS):
            offset = tap * dilation
            ahead_ref[rows, tap * channels : (tap + 1) * channels] = window[
                offset : offset + size
            ].astype(BF16)

    chunks = length // CHUNK
    zero_head = jnp.zeros((TAIL, channels), F32)
    zero_sum = jnp.zeros((8, channels), F32)

    future = right_ref[HALO : 2 * HALO, :].astype(F32) * newest
    put_flow(pl.ds(length, HALO), HALO, future, zero_head, 2 ** (LAYERS - 1))

    def begin(step, carry):
        head, bias_sum = carry
        rows = pl.ds(pl.multiple_of((chunks - 1 - step) * CHUNK, CHUNK), CHUNK)
        flow = cot_ref[rows, :].astype(F32)
        put_flow(rows, CHUNK, flow, head, 2 ** (LAYERS - 1))
        return flow[:TAIL], bias_sum + fold(flow)

    _, bias_sum = lax.fori_loop(0, chunks, begin, (future[:TAIL], zero_sum))

    for layer in reversed(range(LAYERS)):
        small_ref[1, layer : layer + 1, :] = jnp.sum(bias_sum, 0, keepdims=True)
        grads = lax.dot_general(
            act_ref[layer, HALO : HALO + length, :],
            ahead_ref[0:length, :],
            (((0,), (0,)), ((), ())),
            preferred_element_type=F32,
        )
        for tap in range(TAPS):
            for side in range(2):
                at = tap * channels + side * half
                part_ref[layer, side, tap * channels : (tap + 1) * channels, :] = grads[
                    :, at : at + half
                ].astype(BF16)
        advance()
        launch(course(layer))
        back = None
        for tap in range(TAPS):
            one = lax.dot_general(
                ahead_ref[:, tap * channels : (tap + 1) * channels],
                weights_ref[layer, tap * channels : (tap + 1) * channels, :],
                (((1,), (1,)), ((), ())),
                preferred_element_type=F32,
            )
            back = one if back is None else back + one
        back_ref[...] = back
        gain = gain_ref[layer : layer + 1, :]
        below = 2 ** (layer - 1) if layer else None

        def through(start, size, layer=layer, gain=gain):
            rows = pl.ds(start, size)
            held = pl.ds(start + HALO, size)
            normed = normed_ref[layer, held, :]
            rstd = rstd_ref[layer, held, :][:, 0:1]
            a = normed * gain
            squared = a * a
            t = jnp.tanh(CURVE * (a + CUBIC * (squared * a)))
            slope = 0.5 * (1.0 + t) + 0.5 * a * (1.0 - t * t) * (
                CURVE * (1.0 + 3.0 * CUBIC * squared)
            )
            pre = slope * back_ref[rows, :]
            taken = pre * normed
            q = pre * gain
            mean_q = jnp.mean(q, -1, keepdims=True)
            mean_qn = jnp.mean(q * normed, -1, keepdims=True)
            flow = flow_ref[rows, :] + rstd * (q - mean_q - normed * mean_qn)
            return flow, taken

        if layer:
            future, _ = through(length, HALO)
            future = future * newest
            put_flow(pl.ds(length, HALO), HALO, future, zero_head, below)
        else:
            future = zero_head

        def backward(step, carry, layer=layer, below=below, through=through):
            head, bias_sum, gain_sum = carry
            start = pl.multiple_of((chunks - 1 - step) * CHUNK, CHUNK)
            rows = pl.ds(start, CHUNK)
            flow, taken = through(start, CHUNK)
            if layer:
                put_flow(rows, CHUNK, flow, head, below)
            else:
                dhist_ref[rows, :] = flow.astype(BF16)
            return flow[:TAIL], bias_sum + fold(flow), gain_sum + fold(taken)

        _, bias_sum, gain_sum = lax.fori_loop(
            0, chunks, backward, (future[:TAIL], zero_sum, zero_sum)
        )
        small_ref[0, layer : layer + 1, :] = jnp.sum(gain_sum, 0, keepdims=True)

    launch(small_course())
    advance()
    launch(tables_course())
    while running:
        advance()


def body(history, cotangent, weights, ln_gain, conv_bias, pooled_grad, table_owner, row_ids):
    _, length, channels = history.shape
    users, seqs = lax.axis_size("user"), lax.axis_size("seq")
    ys = seqs // 2
    tables = table_owner.shape[0]
    per_owner = tables // users
    lanes = pooled_grad.shape[2]
    block_rows = max(8, 2 * per_owner)
    half = channels // 2
    taken = TAPS * channels
    piece = pl.cdiv(taken, ys * users * 16) * 16
    rows = piece * ys * users
    total = length + 2 * HALO
    vmem = pl.BlockSpec(memory_space=pltpu.VMEM)
    anywhere = pl.BlockSpec(memory_space=pl.ANY)
    small = pltpu.VMEM((2, LAYERS, channels), F32)
    copies = 3 + 2 * (users - 1) + ys + LAYERS * (2 * users + 2 * ys - 2)

    d_history, sums, total_small, table_grad = pl.pallas_call(
        functools.partial(step_kernel, per_owner),
        out_shape=(
            jax.ShapeDtypeStruct((length, channels), BF16),
            jax.ShapeDtypeStruct((LAYERS, 2, taken, half), BF16),
            jax.ShapeDtypeStruct((2, LAYERS, channels), F32),
            jax.ShapeDtypeStruct((per_owner, users, lanes), F32),
        ),
        in_specs=[anywhere] * 8,
        out_specs=(vmem,) * 4,
        scratch_shapes=[
            pltpu.VMEM((length, channels), BF16),
            pltpu.VMEM((length, channels), BF16),
            pltpu.VMEM((LAYERS, taken, channels), BF16),
            pltpu.VMEM((LAYERS, channels), F32),
            pltpu.VMEM((LAYERS, channels), F32),
            pltpu.VMEM((tables, lanes), BF16),
            pltpu.VMEM((1, tables), jnp.int32),
            pltpu.VMEM((1, tables), jnp.int32),
            pltpu.VMEM((HALO, channels), BF16),
            pltpu.VMEM((2 * HALO, channels), BF16),
            pltpu.VMEM((total, channels), F32),
            pltpu.VMEM((LAYERS, total, channels), F32),
            pltpu.VMEM((LAYERS, total, 128), F32),
            pltpu.VMEM((LAYERS, total, channels), BF16),
            pltpu.VMEM((total, taken), BF16),
            pltpu.VMEM((length + HALO, channels), F32),
            pltpu.VMEM((length + HALO, taken), BF16),
            pltpu.VMEM((length + HALO, channels), F32),
            pltpu.VMEM((LAYERS, 2, rows, half), BF16),
            pltpu.VMEM((LAYERS, rows, half), BF16),
            pltpu.VMEM((LAYERS, rows, half), BF16),
            pltpu.VMEM((LAYERS, max(ys - 1, 1), users * piece, half), BF16),
            pltpu.VMEM((LAYERS, users * piece, half), BF16),
            pltpu.VMEM((LAYERS, users - 1, piece, half), BF16),
            pltpu.VMEM((LAYERS, 2, rows, half), BF16),
            small,
            small,
            small,
            pltpu.VMEM((ys, 2, LAYERS, channels), F32),
            small,
            pltpu.VMEM((users, 2, LAYERS, channels), F32),
            pltpu.VMEM((users, block_rows, lanes), F32),
            pltpu.VMEM((users, block_rows, lanes), F32),
            pltpu.SemaphoreType.DMA((8,)),
            pltpu.SemaphoreType.DMA((copies,)),
            pltpu.SemaphoreType.DMA((copies,)),
        ],
        compiler_params=pltpu.CompilerParams(
            collective_id=0, has_side_effects=True, vmem_limit_bytes=60 << 20
        ),
        name="step",
    )(
        history[0], cotangent[0], weights.reshape(LAYERS, taken, channels), ln_gain, conv_bias,
        pooled_grad[0], table_owner.reshape(1, tables), row_ids,
    )

    factor = 1.0 / math.sqrt(users * length * seqs)
    sums = sums.reshape(LAYERS, 2, TAPS, channels, half).astype(F32) * factor
    grad_weights = jnp.concatenate([sums[:, 0], sums[:, 1]], -1)
    total_small = total_small * factor
    return d_history[None], grad_weights, total_small[0], total_small[1], table_grad


def solution(mesh):
    in_specs = (
        P("user", "seq", None),
        P("user", "seq", None),
        P(),
        P(),
        P(),
        P("user", "seq", None),
        P("seq"),
        P("user", "seq"),
    )
    out_specs = (P("user", "seq", None), P(), P(), P(), P(("seq", "user"), None, None))
    return jax.shard_map(body, mesh=mesh, in_specs=in_specs, out_specs=out_specs, check_vma=False)
```

time: 90.3 us -> 66.7 us (0.74)
  the two profiles are of different devices: /device:TPU:31 before, /device:TPU:0 now
where the time goes in v2:
time: 66.7 us; the launch traced here: 66.5 us
  Pallas kernels  59.4 us (89%)
  other arithmetic  4.21 us (6%)
  local copies, waits for them, and re-layouts  2.21 us (3%)
  between operations  0.68 us (1%)
    pallas_call x1, Pallas kernels, body(): pl.pallas_call(functools.partial(step_kernel, per_owner), out_shape=(jax....  59.4 us
    concatenate x1, other arithmetic, body(): grad_weights = jnp.concatenate([sums[:, 0], sums[:, 1]], -1)  1.89 us
    mul x1, other arithmetic, body(): sums = sums.reshape(LAYERS, 2, TAPS, channels, half).astype(F32) * factor  1.62 us

profile of v2, /device:TPU:0, one launch (start us, length us, event | category | flops | bytes accessed | tf_op | source)
XLA Modules:
  0.0 66.5 jit_solution(9547274205565686761)
XLA Ops:
  0.6 59.4 %step.1 = (bf16[512,256]{1,0:T(8,128)(2,1)}, bf16[4,2,768,128]{3,2,1,0:T(8,128)(2,1)}, f32[2,4,256]{2,1,0:T(4,128)}, f32[2,8,128]{2,1,0:T(8,128)}) custom-call(bf16[512,256]{1,0:T(8,128)(2,1)} %bitcast.22, bf16[512,256]{1,0:T(8,128)(2,1)} %bitcast.23, bf16[4,768,256]{2,1,0:T(8,128)(2,1)} %bitcast.20, f32[4,256]{1,0:T(4,128)} %gain_hbm.1, f32[4,256]{1,0:T(4,128)} %bias_hbm.1, ...), custom_call_target="tpu_custom_call" | custom-call | tf_op jit(solution)/shard_map/step/pallas_call | solution.py:412
  60.0 0.7 %broadcast_multiply_fusion = f32[2,4,256]{2,1,0:T(4,128)S(1)} fusion(f32[2,4,256]{2,1,0:T(4,128)} %get-tuple-element.11), kind=kLoop, calls=%fused_computation.6 | loop fusion | flops 2048 | bytes 16384 | tf_op jit(solution)/shard_map/mul | solution.py:472
  60.7 0.6 slice_bitcast_fusion.2
  61.3 1.6 %convert_multiply_fusion = f32[4,2,768,128]{3,2,1,0:T(8,128)S(1)} fusion(bf16[4,2,768,128]{3,2,1,0:T(8,128)(2,1)} %get-tuple-element.10), kind=kLoop, calls=%fused_computation.1 | loop fusion | flops 1572864 | bytes 4718592 | tf_op jit(solution)/shard_map/mul | solution.py:470
  63.0 0.3 slice_bitcast_fusion.1
  63.3 0.0 copy-start
  63.3 0.0 copy-start.1
  63.3 1.9 %pad_maximum_fusion = f32[4,3,256,256]{3,2,1,0:T(8,128)} fusion(f32[4,3,256,128]{3,2,1,0:T(8,128)S(1)} %get-tuple-element.14, f32[4,3,256,128]{3,2,1,0:T(8,128)S(1)} %get-tuple-element.13), kind=kLoop, calls=%fused_computation | loop fusion | flops 786432 | bytes 6291456 | tf_op jit(solution)/shard_map/concatenate | solution.py:471
  65.2 0.0 copy-done
  65.2 0.7 %copy.19 = bf16[1,512,256]{2,1,0:T(8,128)(2,1)} copy(bf16[1,512,256]{2,1,0:T(8,128)(2,1)S(1)} %bitcast.21) | data formatting | bytes 524288
  65.9 0.0 copy-done.1
  65.9 0.6 copy.20
Async XLA Ops:
  63.3 1.9 %copy-start = (bf16[512,256]{1,0:T(8,128)(2,1)S(1)}, bf16[512,256]{1,0:T(8,128)(2,1)}, u32[]{:S(2)}) copy-start(bf16[512,256]{1,0:T(8,128)(2,1)} %get-tuple-element.9) | copy-start | bytes 786436
  63.3 2.6 %copy-start.1 = (f32[2,8,128]{2,1,0:T(8,128)S(1)}, f32[2,8,128]{2,1,0:T(8,128)}, u32[]{:S(2)}) copy-start(f32[2,8,128]{2,1,0:T(8,128)} %get-tuple-element.26) | copy-start | bytes 24580

commit v3 on v2

--- a/solution.py
+++ b/solution.py
@@ -50,7 +50,7 @@
 def step_kernel(
     per_owner,
     hist_hbm, cot_hbm, weights_hbm, gain_hbm, bias_hbm, pooled_hbm, owner_hbm, ids_hbm,
-    dhist_ref, out_ref, total_ref, table_ref,
+    dhist_ref, out_ref, dgain_ref, dbias_ref, table_ref,
     hist_ref, cot_ref, weights_ref, gain_ref, bias_ref, pooled_ref, owner_ref, ids_ref,
     left_ref, right_ref,
     x_ref, normed_ref, rstd_ref, act_ref, shifted_ref, flow_ref, ahead_ref, back_ref,
@@ -65,9 +65,12 @@
     ys = seqs // 2
     half = channels // 2
     rows_all = part_ref.shape[2]
-    piece = rows_all // (ys * users)
+    planes, lines = 2 * ys, users // 2
+    piece = rows_all // (planes * lines)
     seq, user = lax.axis_index("seq"), lax.axis_index("user")
     y, core = seq // 2, seq % 2
+    line, side = user // 2, user % 2
+    plane = y * 2 + side
     sibling = {"seq": y * 2 + 1 - core, "user": user}
     oldest = jnp.where(seq == 0, HALO, 0)
     newest = jnp.where(seq == seqs - 1, 0.0, 1.0).astype(F32)
@@ -94,12 +97,23 @@
         other = lax.rem(user + step, users)
         return other, {"seq": seq, "user": other}
 
+    def of_plane(step):
+        other = lax.rem(plane + step, planes)
+        return other, {"seq": (other // 2) * 2 + core, "user": line * 2 + other % 2}
+
+    def of_line(step):
+        other = lax.rem(line + step, lines)
+        return other, {"seq": seq, "user": other * 2 + side}
+
     barrier = pltpu.get_barrier_semaphore()
     for step in range(1, seqs):
         pl.semaphore_signal(barrier, inc=1, device_id=of_seq(step), device_id_type=MESH)
     for step in range(1, users):
         pl.semaphore_signal(barrier, inc=1, device_id=of_user(step)[1], device_id_type=MESH)
-    pl.semaphore_wait(barrier, seqs + users - 2)
+    for step in range(1, ys):
+        device = {"seq": lax.rem(y + step, ys) * 2 + core, "user": line * 2 + 1 - side}
+        pl.semaphore_signal(barrier, inc=1, device_id=device, device_id_type=MESH)
+    pl.semaphore_wait(barrier, seqs + users + ys - 3)
 
     used = [0]
 
@@ -135,14 +149,14 @@
         other, device = of_user(step)
         table_copies.append(send(blocks_ref.at[other], rows_in.at[user], device))
 
-    def piece_rows(y_index, user_index):
-        return pl.ds(pl.multiple_of((y_index * users + user_index) * piece, 16), piece)
-
-    def y_rows(y_index):
-        return pl.ds(pl.multiple_of(y_index * (users * piece), 16), users * piece)
-
-    def user_rows(user_index):
-        return pl.ds(pl.multiple_of(user_index * piece, 16), piece)
+    def piece_rows(plane_index, line_index):
+        return pl.ds(pl.multiple_of((plane_index * lines + line_index) * piece, 16), piece)
+
+    def plane_rows(plane_index):
+        return pl.ds(pl.multiple_of(plane_index * (lines * piece), 16), lines * piece)
+
+    def line_rows(line_index):
+        return pl.ds(pl.multiple_of(line_index * piece, 16), piece)
 
     def add(first, others):
         summed = first.astype(F32)
@@ -157,34 +171,34 @@
             copy.wait()
         y_send[layer] = add(part_ref[layer, core], [core_recv[layer]])
         flying = []
-        for step in range(1, ys):
-            other, device = of_y(step)
-            flying.append(send(y_send.at[layer, y_rows(other)], y_recv.at[layer, step - 1], device))
+        for step in range(1, planes):
+            other, device = of_plane(step)
+            flying.append(send(y_send.at[layer, plane_rows(other)], y_recv.at[layer, step - 1], device))
         yield
         for copy in flying:
             copy.wait()
         u_send[layer] = add(
-            y_send[layer, y_rows(y), :], [y_recv[layer, step] for step in range(ys - 1)]
+            y_send[layer, plane_rows(plane), :], [y_recv[layer, step] for step in range(planes - 1)]
         )
         flying = []
-        for step in range(1, users):
-            other, device = of_user(step)
+        for step in range(1, lines):
+            other, device = of_line(step)
             flying.append(
-                send(u_send.at[layer, user_rows(other)], u_recv.at[layer, step - 1], device)
+                send(u_send.at[layer, line_rows(other)], u_recv.at[layer, step - 1], device)
             )
         yield
         for copy in flying:
             copy.wait()
-        final[layer, core, piece_rows(y, user), :] = add(
-            u_send[layer, user_rows(user), :], [u_recv[layer, step] for step in range(users - 1)]
+        final[layer, core, piece_rows(plane, line), :] = add(
+            u_send[layer, line_rows(line), :], [u_recv[layer, step] for step in range(lines - 1)]
         )
-        mine = final.at[layer, core, piece_rows(y, user)]
-        flying = [send(mine, mine, of_user(step)[1]) for step in range(1, users)]
-        yield
-        for copy in flying:
-            copy.wait()
-        mine = final.at[layer, core, y_rows(y)]
-        flying = [send(mine, mine, of_y(step)[1]) for step in range(1, ys)]
+        mine = final.at[layer, core, piece_rows(plane, line)]
+        flying = [send(mine, mine, of_line(step)[1]) for step in range(1, lines)]
+        yield
+        for copy in flying:
+            copy.wait()
+        mine = final.at[layer, core, plane_rows(plane)]
+        flying = [send(mine, mine, of_plane(step)[1]) for step in range(1, planes)]
         yield
         for copy in flying:
             copy.wait()
@@ -193,7 +207,11 @@
         yield
         for copy in flying:
             copy.wait()
-        out_ref[layer] = final[layer, :, 0 : TAPS * channels, :]
+        for tap in range(TAPS):
+            for part in range(2):
+                out_ref[layer, tap, :, part * half : (part + 1) * half] = final[
+                    layer, part, tap * channels : (tap + 1) * channels, :
+                ]
 
     def small_course():
         flying = [send(small_ref, small_core, sibling)]
@@ -218,7 +236,9 @@
         small_sum = small_u[0]
         for other in range(1, users):
             small_sum = small_sum + small_u[other]
-        total_ref[...] = small_sum
+        small_sum = small_sum * (1.0 / math.sqrt(users * length * seqs))
+        dgain_ref[...] = small_sum[0]
+        dbias_ref[...] = small_sum[1]
 
     def tables_course():
         rows_in[user] = blocks_ref[user]
@@ -322,12 +342,11 @@
             preferred_element_type=F32,
         )
         for tap in range(TAPS):
-            for side in range(2):
-                at = tap * channels + side * half
-                part_ref[layer, side, tap * channels : (tap + 1) * channels, :] = grads[
+            for part in range(2):
+                at = tap * channels + part * half
+                part_ref[layer, part, tap * channels : (tap + 1) * channels, :] = grads[
                     :, at : at + half
                 ].astype(BF16)
-        advance()
         launch(course(layer))
         back = None
         for tap in range(TAPS):
@@ -339,6 +358,7 @@
             )
             back = one if back is None else back + one
         back_ref[...] = back
+        advance()
         gain = gain_ref[layer : layer + 1, :]
         below = 2 ** (layer - 1) if layer else None
 
@@ -385,6 +405,7 @@
         small_ref[0, layer : layer + 1, :] = jnp.sum(gain_sum, 0, keepdims=True)
 
     launch(small_course())
+    running.reverse()
     advance()
     launch(tables_course())
     while running:
@@ -403,22 +424,24 @@
     taken = TAPS * channels
     piece = pl.cdiv(taken, ys * users * 16) * 16
     rows = piece * ys * users
+    planes, lines = 2 * ys, users // 2
     total = length + 2 * HALO
     vmem = pl.BlockSpec(memory_space=pltpu.VMEM)
     anywhere = pl.BlockSpec(memory_space=pl.ANY)
     small = pltpu.VMEM((2, LAYERS, channels), F32)
-    copies = 3 + 2 * (users - 1) + ys + LAYERS * (2 * users + 2 * ys - 2)
-
-    d_history, sums, total_small, table_grad = pl.pallas_call(
+    copies = 3 + 2 * (users - 1) + ys + LAYERS * (2 * planes + 2 * lines - 2)
+
+    d_history, sums, grad_gain, grad_bias, table_grad = pl.pallas_call(
         functools.partial(step_kernel, per_owner),
         out_shape=(
             jax.ShapeDtypeStruct((length, channels), BF16),
-            jax.ShapeDtypeStruct((LAYERS, 2, taken, half), BF16),
-            jax.ShapeDtypeStruct((2, LAYERS, channels), F32),
+            jax.ShapeDtypeStruct((LAYERS, TAPS, channels, channels), BF16),
+            jax.ShapeDtypeStruct((LAYERS, channels), F32),
+            jax.ShapeDtypeStruct((LAYERS, channels), F32),
             jax.ShapeDtypeStruct((per_owner, users, lanes), F32),
         ),
         in_specs=[anywhere] * 8,
-        out_specs=(vmem,) * 4,
+        out_specs=(vmem,) * 5,
         scratch_shapes=[
             pltpu.VMEM((length, channels), BF16),
             pltpu.VMEM((length, channels), BF16),
@@ -441,9 +464,9 @@
             pltpu.VMEM((LAYERS, 2, rows, half), BF16),
             pltpu.VMEM((LAYERS, rows, half), BF16),
             pltpu.VMEM((LAYERS, rows, half), BF16),
-            pltpu.VMEM((LAYERS, max(ys - 1, 1), users * piece, half), BF16),
-            pltpu.VMEM((LAYERS, users * piece, half), BF16),
-            pltpu.VMEM((LAYERS, users - 1, piece, half), BF16),
+            pltpu.VMEM((LAYERS, planes - 1, lines * piece, half), BF16),
+            pltpu.VMEM((LAYERS, lines * piece, half), BF16),
+            pltpu.VMEM((LAYERS, lines - 1, piece, half), BF16),
             pltpu.VMEM((LAYERS, 2, rows, half), BF16),
             small,
             small,
@@ -467,10 +490,8 @@
     )
 
     factor = 1.0 / math.sqrt(users * length * seqs)
-    sums = sums.reshape(LAYERS, 2, TAPS, channels, half).astype(F32) * factor
-    grad_weights = jnp.concatenate([sums[:, 0], sums[:, 1]], -1)
-    total_small = total_small * factor
-    return d_history[None], grad_weights, total_small[0], total_small[1], table_grad
+    grad_weights = sums.astype(F32) * factor
+    return d_history[None], grad_weights, grad_gain, grad_bias, table_grad
 
 
 def solution(mesh):

time: 66.7 us -> 59.9 us (0.90)
  Pallas kernels: 59.4 us -> 53.1 us
  other arithmetic: 4.21 us -> 3.42 us
    pallas_call x1, Pallas kernels: 59.4 us -> 53.1 us  [body(): pl.pallas_call(functools.partial(step_kernel, per_owner), out_shape=(jax....]
    concatenate x1 -> x0, other arithmetic: 1.89 us -> none  [body(): grad_weights = jnp.concatenate([sums[:, 0], sums[:, 1]], -1)]
    unnamed x6 -> x12, local copies, waits for them, and re-layouts: 1.31 us -> 2.5 us
    mul x2 -> x1, other arithmetic: 2.32 us -> 3.42 us  [body(): grad_weights = sums.astype(F32) * factor]
    squeeze x2 -> x0, local copies, waits for them, and re-layouts: 0.9 us -> none  [the longest x1 0.6 us: body(): total_small[1]]
where the time goes in v3:
time: 59.9 us; the launch traced here: 59.7 us
  Pallas kernels  53.1 us (89%)
  other arithmetic  3.42 us (6%)
  local copies, waits for them, and re-layouts  2.5 us (4%)
  between operations  0.68 us (1%)
    pallas_call x1, Pallas kernels, body(): pl.pallas_call(functools.partial(step_kernel, per_owner), out_shape=(jax....  53.1 us
    mul x1, other arithmetic, body(): grad_weights = sums.astype(F32) * factor  3.42 us
    unnamed x12, local copies, waits for them, and re-layouts  2.5 us

profile of v3, /device:TPU:0, one launch (start us, length us, event | category | flops | bytes accessed | tf_op | source)
XLA Modules:
  0.0 59.7 jit_solution(10451395758458547609)
XLA Ops:
  0.6 53.1 %step.1 = (bf16[512,256]{1,0:T(8,128)(2,1)}, bf16[4,3,256,256]{3,2,1,0:T(8,128)(2,1)}, f32[4,256]{1,0:T(4,128)}, f32[4,256]{1,0:T(4,128)}, f32[2,8,128]{2,1,0:T(8,128)}) custom-call(bf16[512,256]{1,0:T(8,128)(2,1)} %bitcast.8, bf16[512,256]{1,0:T(8,128)(2,1)} %bitcast.9, bf16[4,768,256]{2,1,0:T(8,128)(2,1)} %bitcast.6, f32[4,256]{1,0:T(4,128)} %gain_hbm.1, ...), custom_call_target="tpu_custom_call" | custom-call | tf_op jit(solution)/shard_map/step/pallas_call | solution.py:434
  53.8 0.0 copy-start
  53.8 0.0 copy-start.3
  53.8 0.0 copy-start.2
  53.8 0.0 copy-start.1
  53.8 3.4 %convert_multiply_fusion = f32[4,3,256,256]{3,2,1,0:T(8,128)} fusion(bf16[4,3,256,256]{3,2,1,0:T(8,128)(2,1)} %get-tuple-element.11), kind=kLoop, calls=%fused_computation | loop fusion | flops 1572864 | bytes 4718592 | tf_op jit(solution)/shard_map/mul | solution.py:493
  57.2 0.0 copy-done
  57.2 0.7 %copy.17 = bf16[1,512,256]{2,1,0:T(8,128)(2,1)} copy(bf16[1,512,256]{2,1,0:T(8,128)(2,1)S(1)} %bitcast.7) | data formatting | bytes 524288
  57.9 0.0 copy-done.3
  57.9 0.6 copy.18
  58.5 0.0 copy-done.2
  58.5 0.6 copy.19
  59.1 0.0 copy-done.1
  59.1 0.6 %copy.20 = f32[2,8,128]{2,1,0:T(8,128)} copy(f32[2,8,128]{2,1,0:T(8,128)S(1)} %copy-done.1) | data formatting | bytes 16384
Async XLA Ops:
  53.8 3.5 %copy-start = (bf16[512,256]{1,0:T(8,128)(2,1)S(1)}, bf16[512,256]{1,0:T(8,128)(2,1)}, u32[]{:S(2)}) copy-start(bf16[512,256]{1,0:T(8,128)(2,1)} %get-tuple-element.10) | copy-start | bytes 786436
  53.8 4.2 %copy-start.3 = (f32[4,256]{1,0:T(4,128)S(1)}, f32[4,256]{1,0:T(4,128)}, u32[]{:S(2)}) copy-start(f32[4,256]{1,0:T(4,128)} %get-tuple-element.22) | copy-start | bytes 12292
  53.8 4.7 %copy-start.2 = (f32[4,256]{1,0:T(4,128)S(1)}, f32[4,256]{1,0:T(4,128)}, u32[]{:S(2)}) copy-start(f32[4,256]{1,0:T(4,128)} %get-tuple-element.23) | copy-start | bytes 12292
  53.8 5.3 %copy-start.1 = (f32[2,8,128]{2,1,0:T(8,128)S(1)}, f32[2,8,128]{2,1,0:T(8,128)}, u32[]{:S(2)}) copy-start(f32[2,8,128]{2,1,0:T(8,128)} %get-tuple-element.24) | copy-start | bytes 24580

commit v4 on v3

--- a/solution.py
+++ b/solution.py
@@ -11,7 +11,6 @@
 TAPS = 3
 LAYERS = 4
 HALO = 32
-CHUNK = 64
 TAIL = 16
 EPS = 1e-05
 CURVE = math.sqrt(2.0 / math.pi)
@@ -272,19 +271,22 @@
     x_ref[HALO : HALO + length, :] = hist_ref[...].astype(F32)
     x_ref[HALO + length : total, :] = right_ref[0:HALO, :].astype(F32)
 
+    size_f = next(size for size in (96, 64) if total % size == 0)
+    size_b = next(size for size in (128, 64) if length % size == 0)
+
     for layer in range(LAYERS):
         dilation = 2**layer
         gain = gain_ref[layer : layer + 1, :]
 
         def forward(step, tail, layer=layer, dilation=dilation, gain=gain):
-            start = pl.multiple_of(step * CHUNK, CHUNK)
-            rows = pl.ds(start, CHUNK)
+            start = pl.multiple_of(step * size_f, size_f)
+            rows = pl.ds(start, size_f)
             x = x_ref[rows, :]
             center = x - jnp.mean(x, -1, keepdims=True)
             rstd = lax.rsqrt(jnp.mean(center * center, -1, keepdims=True) + EPS)
             normed = center * rstd
             normed_ref[layer, rows, :] = normed
-            rstd_ref[layer, rows, :] = jnp.broadcast_to(rstd, (CHUNK, 128))
+            rstd_ref[layer, rows, :] = jnp.broadcast_to(rstd, (size_f, 128))
             a = normed * gain
             act = 0.5 * a * (1.0 + jnp.tanh(CURVE * (a + CUBIC * (a * a * a))))
             where = start + lax.broadcasted_iota(jnp.int32, act.shape, 0)
@@ -294,11 +296,11 @@
             for tap in range(TAPS):
                 offset = TAIL - tap * dilation
                 shifted_ref[rows, tap * channels : (tap + 1) * channels] = window[
-                    offset : offset + CHUNK
+                    offset : offset + size_f
                 ].astype(BF16)
-            return act[CHUNK - TAIL :]
-
-        lax.fori_loop(0, total // CHUNK, forward, jnp.zeros((TAIL, channels), F32))
+            return act[size_f - TAIL :]
+
+        lax.fori_loop(0, total // size_f, forward, jnp.zeros((TAIL, channels), F32))
         if layer < LAYERS - 1:
             x_ref[...] = (
                 x_ref[...]
@@ -317,7 +319,7 @@
                 offset : offset + size
             ].astype(BF16)
 
-    chunks = length // CHUNK
+    chunks = length // size_b
     zero_head = jnp.zeros((TAIL, channels), F32)
     zero_sum = jnp.zeros((8, channels), F32)
 
@@ -326,9 +328,9 @@
 
     def begin(step, carry):
         head, bias_sum = carry
-        rows = pl.ds(pl.multiple_of((chunks - 1 - step) * CHUNK, CHUNK), CHUNK)
+        rows = pl.ds(pl.multiple_of((chunks - 1 - step) * size_b, size_b), size_b)
         flow = cot_ref[rows, :].astype(F32)
-        put_flow(rows, CHUNK, flow, head, 2 ** (LAYERS - 1))
+        put_flow(rows, size_b, flow, head, 2 ** (LAYERS - 1))
         return flow[:TAIL], bias_sum + fold(flow)
 
     _, bias_sum = lax.fori_loop(0, chunks, begin, (future[:TAIL], zero_sum))
@@ -390,11 +392,11 @@
 
         def backward(step, carry, layer=layer, below=below, through=through):
             head, bias_sum, gain_sum = carry
-            start = pl.multiple_of((chunks - 1 - step) * CHUNK, CHUNK)
-            rows = pl.ds(start, CHUNK)
-            flow, taken = through(start, CHUNK)
+            start = pl.multiple_of((chunks - 1 - step) * size_b, size_b)
+            rows = pl.ds(start, size_b)
+            flow, taken = through(start, size_b)
             if layer:
-                put_flow(rows, CHUNK, flow, head, below)
+                put_flow(rows, size_b, flow, head, below)
             else:
                 dhist_ref[rows, :] = flow.astype(BF16)
             return flow[:TAIL], bias_sum + fold(flow), gain_sum + fold(taken)
@@ -404,8 +406,8 @@
         )
         small_ref[0, layer : layer + 1, :] = jnp.sum(gain_sum, 0, keepdims=True)
 
+    running.reverse()
     launch(small_course())
-    running.reverse()
     advance()
     launch(tables_course())
     while running:

time: 59.9 us -> 57.6 us (0.962)
  Pallas kernels: 53.1 us -> 50.9 us
    pallas_call x1, Pallas kernels: 53.1 us -> 50.9 us  [body(): pl.pallas_call(functools.partial(step_kernel, per_owner), out_shape=(jax....]
where the time goes in v4:
time: 57.6 us; the launch traced here: 57.5 us
  Pallas kernels  50.9 us (88%)
  other arithmetic  3.42 us (6%)
  local copies, waits for them, and re-layouts  2.5 us (4%)
  between operations  0.68 us (1%)
    pallas_call x1, Pallas kernels, body(): pl.pallas_call(functools.partial(step_kernel, per_owner), out_shape=(jax....  50.9 us
    mul x1, other arithmetic, body(): grad_weights = sums.astype(F32) * factor  3.42 us
    unnamed x12, local copies, waits for them, and re-layouts  2.5 us

profile of v4, /device:TPU:0, one launch (start us, length us, event | category | flops | bytes accessed | tf_op | source)
XLA Modules:
  0.0 57.5 jit_solution(1639439062892021342)
XLA Ops:
  0.6 50.9 %step.1 = (bf16[512,256]{1,0:T(8,128)(2,1)}, bf16[4,3,256,256]{3,2,1,0:T(8,128)(2,1)}, f32[4,256]{1,0:T(4,128)}, f32[4,256]{1,0:T(4,128)}, f32[2,8,128]{2,1,0:T(8,128)}) custom-call(bf16[512,256]{1,0:T(8,128)(2,1)} %bitcast.8, bf16[512,256]{1,0:T(8,128)(2,1)} %bitcast.9, bf16[4,768,256]{2,1,0:T(8,128)(2,1)} %bitcast.6, f32[4,256]{1,0:T(4,128)} %gain_hbm.1, ...), custom_call_target="tpu_custom_call" | custom-call | tf_op jit(solution)/shard_map/step/pallas_call | solution.py:436
  51.5 0.0 copy-start
  51.5 0.0 copy-start.3
  51.5 0.0 copy-start.2
  51.5 0.0 copy-start.1
  51.5 3.4 %convert_multiply_fusion = f32[4,3,256,256]{3,2,1,0:T(8,128)} fusion(bf16[4,3,256,256]{3,2,1,0:T(8,128)(2,1)} %get-tuple-element.11), kind=kLoop, calls=%fused_computation | loop fusion | flops 1572864 | bytes 4718592 | tf_op jit(solution)/shard_map/mul | solution.py:495
  55.0 0.0 copy-done
  55.0 0.7 %copy.17 = bf16[1,512,256]{2,1,0:T(8,128)(2,1)} copy(bf16[1,512,256]{2,1,0:T(8,128)(2,1)S(1)} %bitcast.7) | data formatting | bytes 524288
  55.7 0.0 copy-done.3
  55.7 0.6 %copy.18 = f32[4,256]{1,0:T(4,128)} copy(f32[4,256]{1,0:T(4,128)S(1)} %copy-done.3) | data formatting | bytes 8192
  56.3 0.0 copy-done.2
  56.3 0.6 %copy.19 = f32[4,256]{1,0:T(4,128)} copy(f32[4,256]{1,0:T(4,128)S(1)} %copy-done.2) | data formatting | bytes 8192
  56.9 0.0 copy-done.1
  56.9 0.6 %copy.20 = f32[2,8,128]{2,1,0:T(8,128)} copy(f32[2,8,128]{2,1,0:T(8,128)S(1)} %copy-done.1) | data formatting | bytes 16384
Async XLA Ops:
  51.5 3.5 %copy-start = (bf16[512,256]{1,0:T(8,128)(2,1)S(1)}, bf16[512,256]{1,0:T(8,128)(2,1)}, u32[]{:S(2)}) copy-start(bf16[512,256]{1,0:T(8,128)(2,1)} %get-tuple-element.10) | copy-start | bytes 786436
  51.5 4.2 %copy-start.3 = (f32[4,256]{1,0:T(4,128)S(1)}, f32[4,256]{1,0:T(4,128)}, u32[]{:S(2)}) copy-start(f32[4,256]{1,0:T(4,128)} %get-tuple-element.22) | copy-start | bytes 12292
  51.5 4.7 %copy-start.2 = (f32[4,256]{1,0:T(4,128)S(1)}, f32[4,256]{1,0:T(4,128)}, u32[]{:S(2)}) copy-start(f32[4,256]{1,0:T(4,128)} %get-tuple-element.23) | copy-start | bytes 12292
  51.5 5.3 %copy-start.1 = (f32[2,8,128]{2,1,0:T(8,128)S(1)}, f32[2,8,128]{2,1,0:T(8,128)}, u32[]{:S(2)}) copy-start(f32[2,8,128]{2,1,0:T(8,128)} %get-tuple-element.24) | copy-start | bytes 24580
